TPU v7x, 32 devices: a whole 2x2x4 slice. The times are simulated.
32 devices in a mesh: tm: 4 (over y, core), space: 8 (over z, x).
Axes of the slice: x: 2, y: 2, z: 4, core: 2. Of those that a mesh axis runs over, the one named last changes fastest.
Arguments:
- first_state: float32 [16, 64, 256], P(None, 'space'), may hold values from -6 to 6
- time_embed: float32 [4, 320], P('tm'), may hold values from -6 to 6
- drift_scale: float32 [4], P('tm'), may hold values from 0.05 to 0.25
- state_decay: float32 [4], P('tm'), may hold values from 0.01 to 0.1
- lift_weight: bfloat16 [320, 16], replicated, may hold values from -1.5 to 1.5
- conv_one: bfloat16 [3, 3, 320, 320], replicated, may hold values from -0.109375 to 0.109375
- conv_two: bfloat16 [3, 3, 320, 320], replicated, may hold values from -0.109375 to 0.109375
- project_weight: bfloat16 [16, 320], replicated, may hold values from -0.3125 to 0.3125
Outputs:
- trajectory: float32 [4, 16, 64, 256], P('tm', None, 'space')
All inputs are finite; a program needn't handle non-finite values.
Results may differ from a plain program's by a relative error of at most 0.0019.
Values may be sent and summed in bfloat16 or wider, within the bound.
A program may use at most 128 MiB of HBM per device.

v0:
```python
import functools

import jax
import jax.numpy as jnp
from jax import lax
from jax.experimental import pallas as pl
from jax.experimental.pallas import tpu as pltpu
from jax.sharding import PartitionSpec as P

ITERS = 2
MESH = pl.DeviceIdType.MESH


def silu(v):
    half = 0.5 * v
    return half + half * jnp.tanh(half)


def kernel(
    steps,
    tiles,
    x_hbm,
    embed_hbm,
    scale_ref,
    decay_ref,
    lift_hbm,
    project_hbm,
    conv_one_hbm,
    conv_two_hbm,
    out_ref,
    x_ref,
    embed_ref,
    lift_ref,
    project_ref,
    raw_one,
    raw_two,
    w_one,
    w_two,
    embed_bc,
    lift_rows,
    cols_one,
    cols_two,
    first,
    sums_one,
    sums_two,
    act_three,
    rows_f32,
    state_rows,
    xb_rows,
    drift_out,
    drift_in,
    load_sem,
    halo_send,
    halo_recv,
    drift_send,
    drift_recv,
):
    chans, height, width = x_ref.shape
    feats = lift_ref.shape[1]
    block = 3 * feats
    depth = 3 * block
    chunk = 64 if feats % 64 == 0 else feats
    tm = lax.axis_index("tm")
    space = lax.axis_index("space")
    has_up = space > 0
    has_down = space < tiles - 1

    pairs = (
        (x_hbm, x_ref),
        (embed_hbm, embed_ref),
        (lift_hbm, lift_ref),
        (project_hbm, project_ref),
        (conv_one_hbm, raw_one),
        (conv_two_hbm, raw_two),
    )
    loads = [pltpu.make_async_copy(a, b, load_sem.at[i]) for i, (a, b) in enumerate(pairs)]
    for load in loads:
        load.start()

    barrier = pltpu.get_barrier_semaphore()
    for shift in range(1, steps):
        other = lax.rem(tm + shift, steps)
        pl.semaphore_signal(barrier, inc=1, device_id=(other, space), device_id_type=MESH)

    @pl.when(has_up)
    def _():
        pl.semaphore_signal(barrier, inc=1, device_id=(tm, space - 1), device_id_type=MESH)

    @pl.when(has_down)
    def _():
        pl.semaphore_signal(barrier, inc=1, device_id=(tm, space + 1), device_id_type=MESH)

    def halo_copies(sweep):
        up = pltpu.make_async_remote_copy(
            src_ref=xb_rows.at[sweep, pl.ds(2, 2)],
            dst_ref=xb_rows.at[sweep, pl.ds(height + 2, 2)],
            send_sem=halo_send.at[sweep, 0],
            recv_sem=halo_recv.at[sweep, 1],
            device_id=(tm, space - 1),
            device_id_type=MESH,
        )
        down = pltpu.make_async_remote_copy(
            src_ref=xb_rows.at[sweep, pl.ds(height, 2)],
            dst_ref=xb_rows.at[sweep, pl.ds(0, 2)],
            send_sem=halo_send.at[sweep, 1],
            recv_sem=halo_recv.at[sweep, 0],
            device_id=(tm, space + 1),
            device_id_type=MESH,
        )
        return up, down

    def send_halo(sweep):
        up, down = halo_copies(sweep)

        @pl.when(has_up)
        def _():
            up.start()

        @pl.when(has_down)
        def _():
            down.start()

    def wait_halo(sweep):
        up, down = halo_copies(sweep)

        @pl.when(has_up)
        def _():
            down.wait_recv()

        @pl.when(has_down)
        def _():
            up.wait_recv()

    def drift_copy(sweep, shift, pair):
        return pltpu.make_async_remote_copy(
            src_ref=drift_out.at[sweep, pl.ds(2 * pair, 2)],
            dst_ref=drift_in.at[sweep, shift - 1, pl.ds(2 * pair, 2)],
            send_sem=drift_send.at[sweep, shift - 1, pair],
            recv_sem=drift_recv.at[sweep, shift - 1, pair],
            device_id=(tm + shift, space),
            device_id_type=MESH,
        )

    def send_drift(sweep, pair):
        for shift in range(1, steps):

            @pl.when(tm + shift < steps)
            def _():
                drift_copy(sweep, shift, pair).start()

    def wait_drift(sweep, pair):
        for shift in range(1, steps):

            @pl.when(tm >= shift)
            def _():
                drift_copy(sweep, shift, pair).wait_recv()

    def earlier(sweep, row):
        total = jnp.zeros((chans, width), jnp.float32)
        for shift in range(1, steps):
            total = total + jnp.where(tm >= shift, drift_in[sweep, shift - 1, row], 0.0)
        return total

    lane = lax.broadcasted_iota(jnp.int32, (chunk, width), 1)
    zero = jnp.zeros((), jnp.bfloat16)

    def store_columns(cols, index, start, act):
        base = index * block + start
        mid = act.astype(jnp.bfloat16)
        left = jnp.where(lane == 0, zero, pltpu.roll(mid, 1, 1))
        right = jnp.where(lane == width - 1, zero, pltpu.roll(mid, width - 1, 1))
        cols[base : base + chunk, :] = left
        cols[base + feats : base + feats + chunk, :] = mid
        cols[base + 2 * feats : base + 2 * feats + chunk, :] = right

    def lift(sweep, pair):
        xb = jnp.concatenate([xb_rows[sweep, index] for index in pair], axis=1)
        value = jnp.dot(lift_rows[:, :chans], xb, preferred_element_type=jnp.float32)
        embed = jnp.concatenate([embed_bc[...]] * (width // 128), axis=1)
        for half, index in enumerate(pair):
            first[index] = value[:, half * width : (half + 1) * width] + embed

    def build(index):
        inside = None
        if index < 2:
            inside = has_up
        if index >= height + 2:
            inside = has_down
        for start in range(0, feats, chunk):
            act = silu(first[index, start : start + chunk, :])
            if inside is not None:
                act = jnp.where(inside, act, 0.0)
            store_columns(cols_one, index, start, act)

    def conv_pair(weight, cols, pair):
        taken = [cols[index * block : index * block + depth, :] for index in pair]
        return jnp.dot(
            weight[...], jnp.concatenate(taken, axis=1), preferred_element_type=jnp.float32
        )

    def activate_one(index, slot):
        inside = None
        if index == 0:
            inside = has_up
        if index == height + 1:
            inside = has_down
        for start in range(0, feats, chunk):
            act = silu(sums_one[slot, start : start + chunk, :])
            if inside is not None:
                act = jnp.where(inside, act, 0.0)
            store_columns(cols_two, index, start, act)

    def finish_pair(sweep, pair, slot):
        for start in range(0, feats, chunk):
            for half in range(2):
                act = silu(sums_two[slot + half, start : start + chunk, :])
                act_three[
                    slot // 2, start : start + chunk, half * width : (half + 1) * width
                ] = act.astype(jnp.bfloat16)
        out = jnp.dot(project_ref[...], act_three[slot // 2], preferred_element_type=jnp.float32)
        for half, row in enumerate(pair):
            part = out[:, half * width : (half + 1) * width]
            drift_out[sweep, row] = scale_ref[0] * part - decay_ref[0] * state_rows[row]

    def build_weight(raw, weight, taps=range(9)):
        for tap in taps:
            weight[:, tap * feats : (tap + 1) * feats] = raw[tap // 3, tap % 3]

    def take_states(sweep, pair):
        wait_drift(sweep - 1, pair)
        for row in (2 * pair, 2 * pair + 1):
            state = rows_f32[row] + earlier(sweep - 1, row)
            state_rows[row] = state
            xb_rows[sweep, row + 2] = state.astype(jnp.bfloat16)

    def one_sweep(sweep):
        edges = (0, 1, height - 2, height - 1)
        middle = tuple(range(2, height - 2))

        @pl.when(sweep > 0)
        def _():
            for pair in range(2):
                take_states(sweep, pair)

        for pair in ((2, 3), (4, 5)):
            lift(sweep, pair)
        for index in (2, 3, 4, 5):
            build(index)

        @pl.when(sweep == 0)
        def _():
            loads[4].wait()
            build_weight(raw_one, w_one)

        order = [(index, index + 1) for index in range(2, height, 2)]
        order += [(1, height), (0, height + 1)]
        builds = [(index + 4, index + 5) for index in range(2, height - 2, 2)]
        builds += [(1, height + 2), (0, height + 3), ()]
        before = None
        for turn, pair in enumerate(order):
            fresh = builds[turn]
            if turn == 0:

                @pl.when(sweep > 0)
                def _():
                    for rest in range(height // 2 - 1, 1, -1):
                        take_states(sweep, rest)
                    send_halo(sweep)

            if 1 in fresh:
                wait_halo(sweep)
            if fresh:
                lift(sweep, fresh)
            if turn == len(order) - 2:

                @pl.when(sweep == 0)
                def _():
                    loads[5].wait()

            value = conv_pair(w_one, cols_one, pair)
            if turn == len(order) - 2:
                build_weight(raw_two, w_two, range(2))
            if turn == len(order) - 1:
                build_weight(raw_two, w_two, range(2, 9))
            for index in fresh:
                build(index)
            slot = 2 * (turn % 2)
            if before is not None:
                for half, index in enumerate(before):
                    activate_one(index, 2 - slot + half)
            for half, index in enumerate(pair):
                part = first[index + 1] + value[:, half * width : (half + 1) * width]
                first[index + 1] = part
                sums_one[slot + half] = part
            before, last = pair, slot

        pairs = [middle[:2], edges[:2], edges[2:]]
        pairs += [middle[place : place + 2] for place in range(2, len(middle), 2)]
        done = None
        for turn, pair in enumerate(pairs):
            value = conv_pair(w_two, cols_two, pair)
            slot = 2 * (turn % 2)
            if done is None:
                for half, index in enumerate(before):
                    activate_one(index, last + half)
            else:
                finish_pair(sweep, done, 2 - slot)
            for half, row in enumerate(pair):
                sums_two[slot + half] = (
                    first[row + 2] + value[:, half * width : (half + 1) * width]
                )
            if done is not None:
                send_drift(sweep, done[0] // 2)
            done = pair
        finish_pair(sweep, done, slot)
        send_drift(sweep, done[0] // 2)

    loads[0].wait()
    for row in range(height):
        value = x_ref[:, row, :]
        rows_f32[row] = value
        state_rows[row] = value
        xb_rows[0, row + 2] = value.astype(jnp.bfloat16)
    greeted = (steps - 1) + jnp.where(has_up, 1, 0) + jnp.where(has_down, 1, 0)
    pl.semaphore_wait(barrier, greeted)
    send_halo(0)
    for load in loads[1:4]:
        load.wait()
    wide = (-feats) % 128
    embed_bc[...] = jnp.transpose(
        jnp.pad(jnp.broadcast_to(embed_ref[...], (128, feats)), ((0, 0), (0, wide)))
    )[:feats]
    turned = jnp.transpose(
        jnp.pad(lift_ref[...].astype(jnp.float32), ((0, 128 - chans), (0, wide)))
    )[:feats]
    lift_rows[...] = turned.astype(jnp.bfloat16)

    @pl.loop(0, ITERS)
    def _(sweep):
        one_sweep(sweep)

    for pair in range(height // 2):
        wait_drift(ITERS - 1, pair)
    for row in range(height):
        total = drift_out[ITERS - 1, row] + earlier(ITERS - 1, row)
        out_ref[0, :, row, :] = rows_f32[row] + total

    for sweep in range(ITERS):
        up, down = halo_copies(sweep)

        @pl.when(has_up)
        def _():
            up.wait_send()

        @pl.when(has_down)
        def _():
            down.wait_send()

        for shift in range(1, steps):
            for pair in range(height // 2):

                @pl.when(tm + shift < steps)
                def _():
                    drift_copy(sweep, shift, pair).wait_send()


def solution(mesh):
    steps, tiles = mesh.shape["tm"], mesh.shape["space"]

    def per_device(
        first_state,
        time_embed,
        drift_scale,
        state_decay,
        lift_weight,
        conv_one,
        conv_two,
        project_weight,
    ):
        chans, height, width = first_state.shape
        feats = lift_weight.shape[0]
        block, depth = 3 * feats, 9 * feats
        peers = max(steps - 1, 1)
        vmem = pl.BlockSpec(memory_space=pltpu.VMEM)
        smem = pl.BlockSpec(memory_space=pltpu.SMEM)
        hbm = pl.BlockSpec(memory_space=pltpu.HBM)
        return pl.pallas_call(
            functools.partial(kernel, steps, tiles),
            out_shape=jax.ShapeDtypeStruct((1, chans, height, width), jnp.float32),
            in_specs=[hbm, hbm, smem, smem, hbm, hbm, hbm, hbm],
            out_specs=vmem,
            scratch_shapes=[
                pltpu.VMEM((chans, height, width), jnp.float32),
                pltpu.VMEM((1, feats), jnp.float32),
                pltpu.VMEM((chans, feats), jnp.bfloat16),
                pltpu.VMEM((chans, feats), jnp.bfloat16),
                pltpu.VMEM((3, 3, feats, feats), jnp.bfloat16),
                pltpu.VMEM((3, 3, feats, feats), jnp.bfloat16),
                pltpu.VMEM((feats, depth), jnp.bfloat16),
                pltpu.VMEM((feats, depth), jnp.bfloat16),
                pltpu.VMEM((feats, 128), jnp.float32),
                pltpu.VMEM((feats, 128), jnp.bfloat16),
                pltpu.VMEM(((height + 4) * block, width), jnp.bfloat16),
                pltpu.VMEM(((height + 2) * block, width), jnp.bfloat16),
                pltpu.VMEM((height + 4, feats, width), jnp.float32),
                pltpu.VMEM((4, feats, width), jnp.float32),
                pltpu.VMEM((4, feats, width), jnp.float32),
                pltpu.VMEM((2, feats, 2 * width), jnp.bfloat16),
                pltpu.VMEM((height, chans, width), jnp.float32),
                pltpu.VMEM((height, chans, width), jnp.float32),
                pltpu.VMEM((ITERS, height + 4, chans, width), jnp.bfloat16),
                pltpu.VMEM((ITERS, height, chans, width), jnp.float32),
                pltpu.VMEM((ITERS, peers, height, chans, width), jnp.float32),
                pltpu.SemaphoreType.DMA((6,)),
                pltpu.SemaphoreType.DMA((ITERS, 2)),
                pltpu.SemaphoreType.DMA((ITERS, 2)),
                pltpu.SemaphoreType.DMA((ITERS, peers, height // 2)),
                pltpu.SemaphoreType.DMA((ITERS, peers, height // 2)),
            ],
            compiler_params=pltpu.CompilerParams(
                collective_id=0, has_side_effects=True, vmem_limit_bytes=67043328
            ),
        )(
            first_state,
            time_embed,
            drift_scale,
            state_decay,
            lift_weight.T,
            project_weight,
            conv_one,
            conv_two,
        )

    in_specs = (P(None, "space", None), P("tm", None), P("tm"), P("tm"), P(), P(), P(), P())
    return jax.shard_map(
        per_device,
        mesh=mesh,
        in_specs=in_specs,
        out_specs=P("tm", None, "space", None),
        check_vma=False,
    )
```

profile of v0, /device:TPU:21, one launch (start us, length us, event | category | flops | bytes accessed | tf_op | source)
XLA Modules:
  0.0 35.0 jit_solution(17783385885195890966)
XLA Ops:
  1.3 32.1 %shard_map.82 = f32[1,16,8,256]{3,2,1,0:T(8,128)} custom-call(f32[16,8,256]{2,1,0:T(8,128)} %x_hbm.1, f32[1,320]{1,0:T(1,128)} %embed_hbm.1, f32[1]{0:T(128)S(6)} %copy.10.scale_ref, f32[1]{0:T(128)S(6)} %copy.11.decay_ref, bf16[16,320]{1,0:T(8,128)(2,1)} %bitcast.1, bf16[16,320]{1,0:T(8,128)(2,1)} %project_hbm.1, bf16[3,3,320,320]{3,2,1,0:T(8,128)(2,1)} %conv_one_hbm.1, ...), custom_call_target="tpu_custom_call" | custom-call | tf_op jit(solution)/shard_map/pallas_call | solution.py:387
  33.4 1.6 %copy.12 = f32[1,16,8,256]{3,2,1,0:T(8,128)} copy(f32[1,16,8,256]{3,2,1,0:T(8,128)} %shard_map.82) | data formatting | bytes 262144
where the time goes:
time: 35.2 us; the launch traced here: 35 us
  Pallas kernels  32.1 us (91%)
  local copies, waits for them, and re-layouts  1.57 us (4%)
  between operations  1.3 us (4%)
    pallas_call x1, Pallas kernels, per_device(): pl.pallas_call(functools.partial(kernel, steps, tiles), out_shape=jax.Sha...  32.1 us
    unnamed x1, local copies, waits for them, and re-layouts  1.57 us

commit v1 on v0

v1 whole, which is shorter than its diff:
```python
import functools

import jax
import jax.numpy as jnp
from jax import lax
from jax.experimental import pallas as pl
from jax.experimental.pallas import tpu as pltpu
from jax.sharding import PartitionSpec as P

ITERS = 2
TILE = 256
EXTRA = 64
MESH = pl.DeviceIdType.MESH


def gate(half):
    return half + half * jnp.tanh(half)


def split_three(value):
    high = value.astype(jnp.bfloat16)
    left = value - high.astype(jnp.float32)
    mid = left.astype(jnp.bfloat16)
    low = (left - mid.astype(jnp.float32)).astype(jnp.bfloat16)
    return high, mid, low


def kernel(
    steps,
    tiles,
    x_hbm,
    embed_hbm,
    scale_ref,
    decay_ref,
    lift_hbm,
    project_hbm,
    conv_one_hbm,
    conv_two_hbm,
    out_ref,
    x_ref,
    embed_ref,
    lift_ref,
    project_ref,
    raw_one,
    raw_two,
    u_one,
    u_two,
    lift_rows,
    main_one,
    rest_one,
    main_two,
    rest_two,
    first,
    prods,
    act_three,
    turned,
    rows_f32,
    state_rows,
    xb_rows,
    drift_out,
    drift_in,
    load_sem,
    halo_send,
    halo_recv,
    drift_send,
    drift_recv,
):
    chans, height, width = x_ref.shape
    feats = lift_ref.shape[1]
    side = width // 2
    main = feats // TILE * TILE
    rest = feats - main
    depth = 3 * feats
    chunk = 64
    tm = lax.axis_index("tm")
    space = lax.axis_index("space")
    has_up = space > 0
    has_down = space < tiles - 1

    pairs = (
        (x_hbm, x_ref),
        (embed_hbm, embed_ref),
        (lift_hbm, lift_ref),
        (project_hbm, project_ref),
        (conv_one_hbm, raw_one),
        (conv_two_hbm, raw_two),
    )
    loads = [pltpu.make_async_copy(a, b, load_sem.at[i]) for i, (a, b) in enumerate(pairs)]
    for load in loads:
        load.start()

    barrier = pltpu.get_barrier_semaphore()
    for shift in range(1, steps):
        other = lax.rem(tm + shift, steps)
        pl.semaphore_signal(barrier, inc=1, device_id=(other, space), device_id_type=MESH)

    @pl.when(has_up)
    def _():
        pl.semaphore_signal(barrier, inc=1, device_id=(tm, space - 1), device_id_type=MESH)

    @pl.when(has_down)
    def _():
        pl.semaphore_signal(barrier, inc=1, device_id=(tm, space + 1), device_id_type=MESH)

    def clear_halo(start):
        for sweep in range(ITERS):
            for index in (start, start + 1):
                xb_rows[sweep, index] = jnp.zeros((chans, width), jnp.bfloat16)

    @pl.when(space == 0)
    def _():
        clear_halo(0)

    @pl.when(space == tiles - 1)
    def _():
        clear_halo(height + 2)

    def halo_copies(sweep):
        up = pltpu.make_async_remote_copy(
            src_ref=xb_rows.at[sweep, pl.ds(2, 2)],
            dst_ref=xb_rows.at[sweep, pl.ds(height + 2, 2)],
            send_sem=halo_send.at[sweep, 0],
            recv_sem=halo_recv.at[sweep, 1],
            device_id=(tm, space - 1),
            device_id_type=MESH,
        )
        down = pltpu.make_async_remote_copy(
            src_ref=xb_rows.at[sweep, pl.ds(height, 2)],
            dst_ref=xb_rows.at[sweep, pl.ds(0, 2)],
            send_sem=halo_send.at[sweep, 1],
            recv_sem=halo_recv.at[sweep, 0],
            device_id=(tm, space + 1),
            device_id_type=MESH,
        )
        return up, down

    def send_halo(sweep):
        up, down = halo_copies(sweep)

        @pl.when(has_up)
        def _():
            up.start()

        @pl.when(has_down)
        def _():
            down.start()

    def wait_halo(sweep):
        up, down = halo_copies(sweep)

        @pl.when(has_up)
        def _():
            down.wait_recv()

        @pl.when(has_down)
        def _():
            up.wait_recv()

    def drift_copy(sweep, shift, pair):
        return pltpu.make_async_remote_copy(
            src_ref=drift_out.at[sweep, pl.ds(2 * pair, 2)],
            dst_ref=drift_in.at[sweep, shift - 1, pl.ds(2 * pair, 2)],
            send_sem=drift_send.at[sweep, shift - 1, pair],
            recv_sem=drift_recv.at[sweep, shift - 1, pair],
            device_id=(tm + shift, space),
            device_id_type=MESH,
        )

    def send_drift(sweep, pair):
        for shift in range(1, steps):

            @pl.when(tm + shift < steps)
            def _():
                drift_copy(sweep, shift, pair).start()

    def wait_drift(sweep, pair):
        for shift in range(1, steps):

            @pl.when(tm >= shift)
            def _():
                drift_copy(sweep, shift, pair).wait_recv()

    def earlier(sweep, row):
        total = jnp.zeros((chans, width), jnp.float32)
        for shift in range(1, steps):
            total = total + jnp.where(tm >= shift, drift_in[sweep, shift - 1, row], 0.0)
        return total

    lane = lax.broadcasted_iota(jnp.int32, (chunk, side), 1)
    zero = jnp.zeros((), jnp.bfloat16)
    ones = jnp.ones((EXTRA - chans, side), jnp.bfloat16)

    def spread(mains, rests, index, start, act):
        value = act.astype(jnp.bfloat16)
        even, odd = value[:, :side], value[:, side:]
        before = jnp.where(lane == 0, zero, pltpu.roll(odd, 1, 1))
        after = jnp.where(lane == side - 1, zero, pltpu.roll(even, side - 1, 1))
        parts = (before - odd, even + odd, odd - even, after - even)
        for m, part in enumerate(parts):
            if start < main:
                place = index * main + start
                mains[m, place : place + chunk, :] = part
            else:
                place = index * rest + start - main
                rests[m, place : place + chunk, :] = part

    def extra(sweep, index, odd):
        xb = xb_rows[sweep, index]
        return jnp.concatenate([xb[:, side:] if odd else xb[:, :side], ones], axis=0)

    def product(weight, mains, rests, m, pair, sweep=None):
        taken = []
        used = depth + EXTRA
        for index in pair:
            pieces = [
                mains[m, index * main : (index + 3) * main, :],
                rests[m, index * rest : (index + 3) * rest, :],
            ]
            if sweep is not None and m in (0, 3):
                pieces.append(extra(sweep, index + 1, m == 3))
            else:
                pieces.append(jnp.zeros((EXTRA, side), jnp.bfloat16))
            taken.append(jnp.concatenate(pieces, axis=0))
        return jnp.dot(
            weight[m, :, :used],
            jnp.concatenate(taken, axis=1),
            preferred_element_type=jnp.float32,
        )

    def lift(sweep, pair):
        tall = jnp.ones((128 - chans, 2 * width), jnp.bfloat16)
        xb = jnp.concatenate([xb_rows[sweep, index] for index in pair], axis=1)
        return jnp.dot(
            lift_rows[...],
            jnp.concatenate([xb, tall], axis=0),
            preferred_element_type=jnp.float32,
        )

    def build_items(sweep, pair):
        value = lift(sweep, pair)

        def item(half, index, start):
            act = gate(value[start : start + chunk, half * width : (half + 1) * width])
            if index < 2:
                act = jnp.where(has_up, act, 0.0)
            if index >= height + 2:
                act = jnp.where(has_down, act, 0.0)
            spread(main_one, rest_one, index, start, act)

        return [
            functools.partial(item, half, index, start)
            for half, index in enumerate(pair)
            for start in range(0, feats, chunk)
        ]

    def joined(slot, half, start):
        lanes = slice(half * side, (half + 1) * side)
        m0, m1, m2, m3 = [prods[slot, m, start : start + chunk, lanes] for m in range(4)]
        return jnp.concatenate([m0 + m1 + m2, m1 - m2 + m3], axis=1)

    def activate_items(pair, slot):
        def item(half, index, start):
            value = joined(slot, half, start)
            if 0 < index <= height:
                first[index, start : start + chunk, :] = value
            act = gate(value)
            if index == 0:
                act = jnp.where(has_up, act, 0.0)
            if index == height + 1:
                act = jnp.where(has_down, act, 0.0)
            spread(main_two, rest_two, index, start, act)

        return [
            functools.partial(item, half, index, start)
            for half, index in enumerate(pair)
            for start in range(0, feats, chunk)
        ]

    def finish_items(sweep, pair, slot):
        def item(half, row, start):
            act = gate(first[row + 1, start : start + chunk, :] + joined(slot, half, start))
            act_three[
                slot, start : start + chunk, half * width : (half + 1) * width
            ] = act.astype(jnp.bfloat16)

        def last():
            out = jnp.dot(
                project_ref[...], act_three[slot], preferred_element_type=jnp.float32
            )
            for half, row in enumerate(pair):
                part = out[:, half * width : (half + 1) * width]
                drift_out[sweep, row] = scale_ref[0] * part - decay_ref[0] * state_rows[row]
            send_drift(sweep, pair[0] // 2)

        return [
            functools.partial(item, half, row, start)
            for half, row in enumerate(pair)
            for start in range(0, feats, chunk)
        ] + [last]

    def weight_items(raw, weight):
        def item(p):
            taps = [raw[p, q].astype(jnp.float32) for q in range(3)]
            outer = taps[0] + taps[2]
            filtered = (
                0.5 * taps[0],
                0.25 * (outer + taps[1]),
                0.25 * (outer - taps[1]),
                0.5 * taps[2],
            )
            for m, value in enumerate(filtered):
                value = value.astype(jnp.bfloat16)
                weight[m, :, p * main : (p + 1) * main] = value[:, :main]
                place = 3 * main + p * rest
                weight[m, :, place : place + rest] = value[:, main:]

        return [functools.partial(item, p) for p in range(3)]

    def take_states(sweep, pair):
        wait_drift(sweep - 1, pair)
        for row in (2 * pair, 2 * pair + 1):
            state = rows_f32[row] + earlier(sweep - 1, row)
            state_rows[row] = state
            xb_rows[sweep, row + 2] = state.astype(jnp.bfloat16)

    def run(items):
        for item in items:
            item()

    def turn(slot, products, items):
        count = len(products)
        for m, make in enumerate(products):
            prods[slot, m] = make()
            run(items[m * len(items) // count : (m + 1) * len(items) // count])

    def one_sweep(sweep):
        if sweep > 0:
            for pair in range(2):
                take_states(sweep, pair)
        run(build_items(sweep, (2, 3)))
        run(build_items(sweep, (4, 5)))
        if sweep == 0:
            loads[4].wait()
            run(weight_items(raw_one, u_one))

        order = [(index, index + 1) for index in range(2, height, 2)]
        order += [(1, height), (0, height + 1)]
        builds = [(index + 4, index + 5) for index in range(2, height - 2, 2)]
        builds += [(1, height + 2), (0, height + 3), ()]
        before = None
        for place, pair in enumerate(order):
            fresh = builds[place]
            items = []
            if place == 0 and sweep > 0:
                for rest_pair in range(height // 2 - 1, 1, -1):
                    take_states(sweep, rest_pair)
                send_halo(sweep)
            if 1 in fresh:
                wait_halo(sweep)
            if fresh:
                items += build_items(sweep, fresh)
            if before is not None:
                items += activate_items(before, 1 - place % 2)
            if sweep == 0 and place == 1:
                loads[5].wait()
            if sweep == 0 and place >= 1:
                items += weight_items(raw_two, u_two)[place - 1 : place]
            turn(
                place % 2,
                [
                    functools.partial(product, u_one, main_one, rest_one, m, pair, sweep)
                    for m in range(4)
                ],
                items,
            )
            before, slot = pair, place % 2

        edges = (0, 1, height - 2, height - 1)
        middle = tuple(range(2, height - 2))
        order = [middle[:2], edges[:2], edges[2:]]
        order += [middle[place : place + 2] for place in range(2, len(middle), 2)]
        done = None
        for pair in order:
            if done is None:
                items = activate_items(before, slot)
            else:
                items = finish_items(sweep, done, slot)
            slot = 1 - slot
            turn(
                slot,
                [
                    functools.partial(product, u_two, main_two, rest_two, m, pair)
                    for m in range(4)
                ],
                items,
            )
            done = pair
        run(finish_items(sweep, done, slot))

    def parted(out_of):
        down = lax.broadcasted_iota(jnp.int32, (width, width), 0)
        across = lax.broadcasted_iota(jnp.int32, (width, width), 1)
        place, column = (down, across) if out_of else (across, down)
        source = jnp.where(place < side, 2 * place, 2 * (place - side) + 1)
        return jnp.where(source == column, 1.0, 0.0).astype(jnp.bfloat16)

    def reorder(value, matrix):
        return jnp.dot(
            jnp.concatenate(split_three(value), axis=1),
            jnp.concatenate([matrix] * 3, axis=0),
            preferred_element_type=jnp.float32,
        )

    into = parted(False)
    loads[0].wait()
    ordered = reorder(x_ref[...].reshape(chans * height, width), into)
    turned[...] = ordered.reshape(chans, height, width)
    for row in range(height):
        value = turned[:, row, :]
        rows_f32[row] = value
        state_rows[row] = value
        xb_rows[0, row + 2] = value.astype(jnp.bfloat16)
    greeted = (steps - 1) + jnp.where(has_up, 1, 0) + jnp.where(has_down, 1, 0)
    pl.semaphore_wait(barrier, greeted)
    send_halo(0)
    for load in loads[1:4]:
        load.wait()
    wide = (-feats) % 128
    parts = [
        part.astype(jnp.float32)
        for part in split_three(jnp.pad(embed_ref[...], ((0, 0), (0, wide))))
    ]
    line = lax.broadcasted_iota(jnp.int32, (128 - chans, feats + wide), 0)
    under = jnp.zeros((128 - chans, feats + wide), jnp.float32)
    for place, part in enumerate(parts):
        under = jnp.where(line == place, part, under)
    over = jnp.pad(lift_ref[...].astype(jnp.float32), ((0, 0), (0, wide)))
    stacked = jnp.transpose(jnp.concatenate([over, under], axis=0))[:feats]
    lift_rows[...] = (0.5 * stacked).astype(jnp.bfloat16)
    for m in range(4):
        none = jnp.zeros((feats, EXTRA), jnp.bfloat16)
        u_one[m, :, depth : depth + EXTRA] = lift_rows[:, :EXTRA] if m in (0, 3) else none
        u_two[m, :, depth : depth + EXTRA] = none

    for sweep in range(ITERS):
        one_sweep(sweep)

    for pair in range(height // 2):
        wait_drift(ITERS - 1, pair)
    for row in range(height):
        turned[:, row, :] = drift_out[ITERS - 1, row] + earlier(ITERS - 1, row)
    total = reorder(turned[...].reshape(chans * height, width), parted(True))
    out_ref[0] = x_ref[...] + total.reshape(chans, height, width)

    for sweep in range(ITERS):
        up, down = halo_copies(sweep)

        @pl.when(has_up)
        def _():
            up.wait_send()

        @pl.when(has_down)
        def _():
            down.wait_send()

        for shift in range(1, steps):
            for pair in range(height // 2):

                @pl.when(tm + shift < steps)
                def _():
                    drift_copy(sweep, shift, pair).wait_send()


def solution(mesh):
    steps, tiles = mesh.shape["tm"], mesh.shape["space"]

    def per_device(
        first_state,
        time_embed,
        drift_scale,
        state_decay,
        lift_weight,
        conv_one,
        conv_two,
        project_weight,
    ):
        chans, height, width = first_state.shape
        feats = lift_weight.shape[0]
        main = feats // TILE * TILE
        rest = feats - main
        depth = 3 * feats
        side = width // 2
        lines = pl.cdiv(depth + EXTRA, 128)
        wide = (lines + 1 - lines % 2) * 128
        peers = max(steps - 1, 1)
        vmem = pl.BlockSpec(memory_space=pltpu.VMEM)
        smem = pl.BlockSpec(memory_space=pltpu.SMEM)
        hbm = pl.BlockSpec(memory_space=pltpu.HBM)
        return pl.pallas_call(
            functools.partial(kernel, steps, tiles),
            out_shape=jax.ShapeDtypeStruct((1, chans, height, width), jnp.float32),
            in_specs=[hbm, hbm, smem, smem, hbm, hbm, hbm, hbm],
            out_specs=vmem,
            scratch_shapes=[
                pltpu.VMEM((chans, height, width), jnp.float32),
                pltpu.VMEM((1, feats), jnp.float32),
                pltpu.VMEM((chans, feats), jnp.bfloat16),
                pltpu.VMEM((chans, feats), jnp.bfloat16),
                pltpu.VMEM((3, 3, feats, feats), jnp.bfloat16),
                pltpu.VMEM((3, 3, feats, feats), jnp.bfloat16),
                pltpu.VMEM((4, feats, wide), jnp.bfloat16),
                pltpu.VMEM((4, feats, wide), jnp.bfloat16),
                pltpu.VMEM((feats, 128), jnp.bfloat16),
                pltpu.VMEM((4, (height + 4) * main, side), jnp.bfloat16),
                pltpu.VMEM((4, (height + 4) * rest, side), jnp.bfloat16),
                pltpu.VMEM((4, (height + 2) * main, side), jnp.bfloat16),
                pltpu.VMEM((4, (height + 2) * rest, side), jnp.bfloat16),
                pltpu.VMEM((height + 2, feats, width), jnp.float32),
                pltpu.VMEM((2, 4, feats, width), jnp.float32),
                pltpu.VMEM((2, feats, 2 * width), jnp.bfloat16),
                pltpu.VMEM((chans, height, width), jnp.float32),
                pltpu.VMEM((height, chans, width), jnp.float32),
                pltpu.VMEM((height, chans, width), jnp.float32),
                pltpu.VMEM((ITERS, height + 4, chans, width), jnp.bfloat16),
                pltpu.VMEM((ITERS, height, chans, width), jnp.float32),
                pltpu.VMEM((ITERS, peers, height, chans, width), jnp.float32),
                pltpu.SemaphoreType.DMA((6,)),
                pltpu.SemaphoreType.DMA((ITERS, 2)),
                pltpu.SemaphoreType.DMA((ITERS, 2)),
                pltpu.SemaphoreType.DMA((ITERS, peers, height // 2)),
                pltpu.SemaphoreType.DMA((ITERS, peers, height // 2)),
            ],
            compiler_params=pltpu.CompilerParams(
                collective_id=0, has_side_effects=True, vmem_limit_bytes=67043328
            ),
        )(
            first_state,
            time_embed,
            drift_scale,
            state_decay,
            lift_weight.T,
            project_weight,
            conv_one,
            conv_two,
        )

    in_specs = (P(None, "space", None), P("tm", None), P("tm"), P("tm"), P(), P(), P(), P())
    return jax.shard_map(
        per_device,
        mesh=mesh,
        in_specs=in_specs,
        out_specs=P("tm", None, "space", None),
        check_vma=False,
    )
```

time: 35.2 us -> 31.2 us (0.89)
  Pallas kernels: 32.1 us -> 28.1 us
    pallas_call x1, Pallas kernels: 32.1 us -> 28.1 us  [per_device(): pl.pallas_call(functools.partial(kernel, steps, tiles), out_shape=jax.Sha...]
where the time goes in v1:
time: 31.2 us; the launch traced here: 31 us
  Pallas kernels  28.1 us (90%)
  local copies, waits for them, and re-layouts  1.57 us (5%)
  between operations  1.31 us (4%)
    pallas_call x1, Pallas kernels, per_device(): pl.pallas_call(functools.partial(kernel, steps, tiles), out_shape=jax.Sha...  28.1 us
    unnamed x1, local copies, waits for them, and re-layouts  1.57 us

profile of v1, /device:TPU:21, one launch (start us, length us, event | category | flops | bytes accessed | tf_op | source)
XLA Modules:
  0.0 31.0 jit_solution(8091729370743335468)
XLA Ops:
  1.3 28.1 %shard_map.82 = f32[1,16,8,256]{3,2,1,0:T(8,128)} custom-call(f32[16,8,256]{2,1,0:T(8,128)} %x_hbm.1, f32[1,320]{1,0:T(1,128)} %embed_hbm.1, f32[1]{0:T(128)S(6)} %copy.10.scale_ref, f32[1]{0:T(128)S(6)} %copy.11.decay_ref, bf16[16,320]{1,0:T(8,128)(2,1)} %bitcast.1, bf16[16,320]{1,0:T(8,128)(2,1)} %project_hbm.1, bf16[3,3,320,320]{3,2,1,0:T(8,128)(2,1)} %conv_one_hbm.1, ...), custom_call_target="tpu_custom_call" | custom-call | tf_op jit(solution)/shard_map/pallas_call | solution.py:499
  29.4 1.6 %copy.12 = f32[1,16,8,256]{3,2,1,0:T(8,128)} copy(f32[1,16,8,256]{3,2,1,0:T(8,128)} %shard_map.82) | data formatting | bytes 262144

commit v2 on v1

--- a/solution.py
+++ b/solution.py
@@ -57,6 +57,7 @@
     rows_f32,
     state_rows,
     xb_rows,
+    drift_own,
     drift_out,
     drift_in,
     load_sem,
@@ -77,16 +78,12 @@
     has_up = space > 0
     has_down = space < tiles - 1
 
-    pairs = (
-        (x_hbm, x_ref),
-        (embed_hbm, embed_ref),
-        (lift_hbm, lift_ref),
-        (project_hbm, project_ref),
-        (conv_one_hbm, raw_one),
-        (conv_two_hbm, raw_two),
-    )
+    pairs = [(x_hbm, x_ref), (embed_hbm, embed_ref), (lift_hbm, lift_ref)]
+    pairs += [(project_hbm, project_ref)]
+    pairs += [(conv_one_hbm.at[p], raw_one.at[p]) for p in range(3)]
+    pairs += [(conv_two_hbm.at[p], raw_two.at[p]) for p in range(3)]
     loads = [pltpu.make_async_copy(a, b, load_sem.at[i]) for i, (a, b) in enumerate(pairs)]
-    for load in loads:
+    for load in loads[:7]:
         load.start()
 
     barrier = pltpu.get_barrier_semaphore()
@@ -134,27 +131,15 @@
         )
         return up, down
 
-    def send_halo(sweep):
-        up, down = halo_copies(sweep)
-
+    def send_up(sweep):
         @pl.when(has_up)
         def _():
-            up.start()
-
+            halo_copies(sweep)[0].start()
+
+    def send_down(sweep):
         @pl.when(has_down)
         def _():
-            down.start()
-
-    def wait_halo(sweep):
-        up, down = halo_copies(sweep)
-
-        @pl.when(has_up)
-        def _():
-            down.wait_recv()
-
-        @pl.when(has_down)
-        def _():
-            up.wait_recv()
+            halo_copies(sweep)[1].start()
 
     def drift_copy(sweep, shift, pair):
         return pltpu.make_async_remote_copy(
@@ -183,16 +168,16 @@
     def earlier(sweep, row):
         total = jnp.zeros((chans, width), jnp.float32)
         for shift in range(1, steps):
-            total = total + jnp.where(tm >= shift, drift_in[sweep, shift - 1, row], 0.0)
+            part = drift_in[sweep, shift - 1, row].astype(jnp.float32)
+            total = total + jnp.where(tm >= shift, part, 0.0)
         return total
 
     lane = lax.broadcasted_iota(jnp.int32, (chunk, side), 1)
     zero = jnp.zeros((), jnp.bfloat16)
     ones = jnp.ones((EXTRA - chans, side), jnp.bfloat16)
 
-    def spread(mains, rests, index, start, act):
-        value = act.astype(jnp.bfloat16)
-        even, odd = value[:, :side], value[:, side:]
+    def spread(mains, rests, index, start, even, odd):
+        even, odd = even.astype(jnp.bfloat16), odd.astype(jnp.bfloat16)
         before = jnp.where(lane == 0, zero, pltpu.roll(odd, 1, 1))
         after = jnp.where(lane == side - 1, zero, pltpu.roll(even, side - 1, 1))
         parts = (before - odd, even + odd, odd - even, after - even)
@@ -237,15 +222,49 @@
         )
 
     def build_items(sweep, pair):
-        value = lift(sweep, pair)
+        held = []
+
+        def first_item():
+            for index in pair:
+                reach(sweep, index)
+            held.append(lift(sweep, pair))
 
         def item(half, index, start):
-            act = gate(value[start : start + chunk, half * width : (half + 1) * width])
-            if index < 2:
-                act = jnp.where(has_up, act, 0.0)
-            if index >= height + 2:
-                act = jnp.where(has_down, act, 0.0)
-            spread(main_one, rest_one, index, start, act)
+            acts = []
+            for lanes in (half * width, half * width + side):
+                act = gate(held[0][start : start + chunk, lanes : lanes + side])
+                if index < 2:
+                    act = jnp.where(has_up, act, 0.0)
+                if index >= height + 2:
+                    act = jnp.where(has_down, act, 0.0)
+                acts.append(act)
+            spread(main_one, rest_one, index, start, *acts)
+
+        return [first_item] + [
+            functools.partial(item, half, index, start)
+            for half, index in enumerate(pair)
+            for start in range(0, feats, chunk)
+        ]
+
+    def joined(slot, half, start):
+        lanes = slice(half * side, (half + 1) * side)
+        m0, m1, m2, m3 = [prods[slot, m, start : start + chunk, lanes] for m in range(4)]
+        return m0 + m1 + m2, m1 - m2 + m3
+
+    def activate_items(sweep, pair, slot):
+        def item(half, index, start):
+            values = joined(slot, half, start)
+            acts = []
+            for place, value in enumerate(values):
+                if 0 < index <= height:
+                    first[index, start : start + chunk, place * side : (place + 1) * side] = value
+                act = gate(value)
+                if index == 0:
+                    act = jnp.where(has_up, act, 0.0)
+                if index == height + 1:
+                    act = jnp.where(has_down, act, 0.0)
+                acts.append(act)
+            spread(main_two, rest_two, index, start, *acts)
 
         return [
             functools.partial(item, half, index, start)
@@ -253,35 +272,13 @@
             for start in range(0, feats, chunk)
         ]
 
-    def joined(slot, half, start):
-        lanes = slice(half * side, (half + 1) * side)
-        m0, m1, m2, m3 = [prods[slot, m, start : start + chunk, lanes] for m in range(4)]
-        return jnp.concatenate([m0 + m1 + m2, m1 - m2 + m3], axis=1)
-
-    def activate_items(pair, slot):
-        def item(half, index, start):
-            value = joined(slot, half, start)
-            if 0 < index <= height:
-                first[index, start : start + chunk, :] = value
-            act = gate(value)
-            if index == 0:
-                act = jnp.where(has_up, act, 0.0)
-            if index == height + 1:
-                act = jnp.where(has_down, act, 0.0)
-            spread(main_two, rest_two, index, start, act)
-
-        return [
-            functools.partial(item, half, index, start)
-            for half, index in enumerate(pair)
-            for start in range(0, feats, chunk)
-        ]
-
     def finish_items(sweep, pair, slot):
         def item(half, row, start):
-            act = gate(first[row + 1, start : start + chunk, :] + joined(slot, half, start))
-            act_three[
-                slot, start : start + chunk, half * width : (half + 1) * width
-            ] = act.astype(jnp.bfloat16)
+            for place, value in enumerate(joined(slot, half, start)):
+                lanes = slice(place * side, (place + 1) * side)
+                act = gate(first[row + 1, start : start + chunk, lanes] + value)
+                lanes = slice(half * width + place * side, half * width + (place + 1) * side)
+                act_three[slot, start : start + chunk, lanes] = act.astype(jnp.bfloat16)
 
         def last():
             out = jnp.dot(
@@ -289,7 +286,10 @@
             )
             for half, row in enumerate(pair):
                 part = out[:, half * width : (half + 1) * width]
-                drift_out[sweep, row] = scale_ref[0] * part - decay_ref[0] * state_rows[row]
+                drift = scale_ref[0] * part - decay_ref[0] * state_rows[row]
+                drift_out[sweep, row] = drift.astype(jnp.bfloat16)
+                if sweep == ITERS - 1:
+                    drift_own[row] = drift
             send_drift(sweep, pair[0] // 2)
 
         return [
@@ -298,8 +298,9 @@
             for start in range(0, feats, chunk)
         ] + [last]
 
-    def weight_items(raw, weight):
+    def weight_items(raw, weight, number):
         def item(p):
+            loads[number + p].wait()
             taps = [raw[p, q].astype(jnp.float32) for q in range(3)]
             outer = taps[0] + taps[2]
             filtered = (
@@ -316,86 +317,123 @@
 
         return [functools.partial(item, p) for p in range(3)]
 
-    def take_states(sweep, pair):
-        wait_drift(sweep - 1, pair)
-        for row in (2 * pair, 2 * pair + 1):
-            state = rows_f32[row] + earlier(sweep - 1, row)
-            state_rows[row] = state
-            xb_rows[sweep, row + 2] = state.astype(jnp.bfloat16)
+    reached = set()
+
+    def reach(sweep, index):
+        if index < 2:
+            key = (sweep, "up")
+        elif index >= height + 2:
+            key = (sweep, "down")
+        else:
+            key = (sweep, index // 2 - 1)
+        if key in reached:
+            return
+        reached.add(key)
+        if index < 2:
+
+            @pl.when(has_up)
+            def _():
+                halo_copies(sweep)[1].wait_recv()
+
+        elif index >= height + 2:
+
+            @pl.when(has_down)
+            def _():
+                halo_copies(sweep)[0].wait_recv()
+
+        elif sweep > 0:
+            pair = key[1]
+            wait_drift(sweep - 1, pair)
+            for row in (2 * pair, 2 * pair + 1):
+                state = rows_f32[row] + earlier(sweep - 1, row)
+                state_rows[row] = state
+                xb_rows[sweep, row + 2] = state.astype(jnp.bfloat16)
+            if pair == 0:
+                send_up(sweep)
+            if pair == height // 2 - 1:
+                send_down(sweep)
 
     def run(items):
         for item in items:
             item()
 
-    def turn(slot, products, items):
+    def turn(slot, products, early, late):
         count = len(products)
+        shares = [[] for _ in products]
+        for place, item in enumerate(early):
+            shares[place * (count - 1) // len(early)].append(item)
+        for place, item in enumerate(late):
+            shares[count // 2 + place * (count // 2) // len(late)].append(item)
         for m, make in enumerate(products):
             prods[slot, m] = make()
-            run(items[m * len(items) // count : (m + 1) * len(items) // count])
-
-    def one_sweep(sweep):
-        if sweep > 0:
-            for pair in range(2):
-                take_states(sweep, pair)
-        run(build_items(sweep, (2, 3)))
-        run(build_items(sweep, (4, 5)))
-        if sweep == 0:
-            loads[4].wait()
-            run(weight_items(raw_one, u_one))
-
-        order = [(index, index + 1) for index in range(2, height, 2)]
-        order += [(1, height), (0, height + 1)]
-        builds = [(index + 4, index + 5) for index in range(2, height - 2, 2)]
-        builds += [(1, height + 2), (0, height + 3), ()]
-        before = None
-        for place, pair in enumerate(order):
-            fresh = builds[place]
-            items = []
-            if place == 0 and sweep > 0:
-                for rest_pair in range(height // 2 - 1, 1, -1):
-                    take_states(sweep, rest_pair)
-                send_halo(sweep)
-            if 1 in fresh:
-                wait_halo(sweep)
-            if fresh:
-                items += build_items(sweep, fresh)
-            if before is not None:
-                items += activate_items(before, 1 - place % 2)
-            if sweep == 0 and place == 1:
-                loads[5].wait()
-            if sweep == 0 and place >= 1:
-                items += weight_items(raw_two, u_two)[place - 1 : place]
-            turn(
-                place % 2,
-                [
+            run(shares[m])
+
+    def plan():
+        top = height // 2 - 1
+        middle = [("A", (index, index + 1)) for index in range(2, height, 2)]
+        inner = [("B", pair) for pair in range(1, top)]
+        ends = [("A", (0, 1)), ("A", (height, height + 1)), ("B", 0), ("B", top)]
+        swapped = [ends[1], ends[0], ends[3], ends[2]]
+        again = middle[1:2] + middle[:1] + middle[2:]
+        return [(0, *part) for part in middle + inner + ends] + [
+            (sweep, *part) for sweep in range(1, ITERS) for part in again + inner + swapped
+        ]
+
+    def all_turns():
+        turns = plan()
+        built = set()
+
+        def missing(place):
+            if place >= len(turns) or turns[place][1] != "A":
+                return []
+            sweep, _, pair = turns[place]
+            rows = [index for index in range(pair[0], pair[1] + 3)]
+            found = []
+            for index in rows:
+                both = (index - index % 2, index - index % 2 + 1)
+                if (sweep, both) not in built:
+                    built.add((sweep, both))
+                    found.append((sweep, both))
+            return found
+
+        for sweep, pair in missing(0):
+            run(build_items(sweep, pair))
+        run(weight_items(raw_one, u_one, 4))
+        after = []
+        waiting = []
+        for place, (sweep, kind, pair) in enumerate(turns):
+            slot = place % 2
+            for missed in missing(place):
+                run(build_items(*missed))
+            late = []
+            for coming in missing(place + 1):
+                late += build_items(*coming)
+            if place == 0:
+                waiting = weight_items(raw_two, u_two, 7)
+                loads[7].start()
+                loads[8].start()
+                loads[9].start()
+            elif place + 1 < len(turns) and turns[place + 1][1] == "B":
+                late, waiting = late + waiting, []
+            else:
+                late, waiting = late + waiting[:1], waiting[1:]
+            if kind == "A":
+                products = [
                     functools.partial(product, u_one, main_one, rest_one, m, pair, sweep)
                     for m in range(4)
-                ],
-                items,
-            )
-            before, slot = pair, place % 2
-
-        edges = (0, 1, height - 2, height - 1)
-        middle = tuple(range(2, height - 2))
-        order = [middle[:2], edges[:2], edges[2:]]
-        order += [middle[place : place + 2] for place in range(2, len(middle), 2)]
-        done = None
-        for pair in order:
-            if done is None:
-                items = activate_items(before, slot)
+                ]
             else:
-                items = finish_items(sweep, done, slot)
-            slot = 1 - slot
-            turn(
-                slot,
-                [
-                    functools.partial(product, u_two, main_two, rest_two, m, pair)
+                rows = (2 * pair, 2 * pair + 1)
+                products = [
+                    functools.partial(product, u_two, main_two, rest_two, m, rows)
                     for m in range(4)
-                ],
-                items,
-            )
-            done = pair
-        run(finish_items(sweep, done, slot))
+                ]
+            turn(slot, products, after, late)
+            if kind == "A":
+                after = activate_items(sweep, pair, slot)
+            else:
+                after = finish_items(sweep, rows, slot)
+        run(after)
 
     def parted(out_of):
         down = lax.broadcasted_iota(jnp.int32, (width, width), 0)
@@ -422,7 +460,8 @@
         xb_rows[0, row + 2] = value.astype(jnp.bfloat16)
     greeted = (steps - 1) + jnp.where(has_up, 1, 0) + jnp.where(has_down, 1, 0)
     pl.semaphore_wait(barrier, greeted)
-    send_halo(0)
+    send_up(0)
+    send_down(0)
     for load in loads[1:4]:
         load.wait()
     wide = (-feats) % 128
@@ -442,13 +481,12 @@
         u_one[m, :, depth : depth + EXTRA] = lift_rows[:, :EXTRA] if m in (0, 3) else none
         u_two[m, :, depth : depth + EXTRA] = none
 
-    for sweep in range(ITERS):
-        one_sweep(sweep)
+    all_turns()
 
     for pair in range(height // 2):
         wait_drift(ITERS - 1, pair)
     for row in range(height):
-        turned[:, row, :] = drift_out[ITERS - 1, row] + earlier(ITERS - 1, row)
+        turned[:, row, :] = drift_own[row] + earlier(ITERS - 1, row)
     total = reorder(turned[...].reshape(chans * height, width), parted(True))
     out_ref[0] = x_ref[...] + total.reshape(chans, height, width)
 
@@ -522,9 +560,10 @@
                 pltpu.VMEM((height, chans, width), jnp.float32),
                 pltpu.VMEM((height, chans, width), jnp.float32),
                 pltpu.VMEM((ITERS, height + 4, chans, width), jnp.bfloat16),
-                pltpu.VMEM((ITERS, height, chans, width), jnp.float32),
-                pltpu.VMEM((ITERS, peers, height, chans, width), jnp.float32),
-                pltpu.SemaphoreType.DMA((6,)),
+                pltpu.VMEM((height, chans, width), jnp.float32),
+                pltpu.VMEM((ITERS, height, chans, width), jnp.bfloat16),
+                pltpu.VMEM((ITERS, peers, height, chans, width), jnp.bfloat16),
+                pltpu.SemaphoreType.DMA((10,)),
                 pltpu.SemaphoreType.DMA((ITERS, 2)),
                 pltpu.SemaphoreType.DMA((ITERS, 2)),
                 pltpu.SemaphoreType.DMA((ITERS, peers, height // 2)),

time: 31.2 us -> 29.3 us (0.939)
  Pallas kernels: 28.1 us -> 26.1 us
    pallas_call x1, Pallas kernels: 28.1 us -> 26.1 us  [per_device(): pl.pallas_call(functools.partial(kernel, steps, tiles), out_shape=jax.Sha...]
where the time goes in v2:
time: 29.3 us; the launch traced here: 29 us
  Pallas kernels  26.1 us (89%)
  local copies, waits for them, and re-layouts  1.57 us (5%)
  between operations  1.31 us (4%)
    pallas_call x1, Pallas kernels, per_device(): pl.pallas_call(functools.partial(kernel, steps, tiles), out_shape=jax.Sha...  26.1 us
    unnamed x1, local copies, waits for them, and re-layouts  1.57 us

profile of v2, /device:TPU:21, one launch (start us, length us, event | category | flops | bytes accessed | tf_op | source)
XLA Modules:
  0.0 29.0 jit_solution(12609586602516284412)
XLA Ops:
  1.3 26.1 %shard_map.82 = f32[1,16,8,256]{3,2,1,0:T(8,128)} custom-call(f32[16,8,256]{2,1,0:T(8,128)} %x_hbm.1, f32[1,320]{1,0:T(1,128)} %embed_hbm.1, f32[1]{0:T(128)S(6)} %copy.10.scale_ref, f32[1]{0:T(128)S(6)} %copy.11.decay_ref, bf16[16,320]{1,0:T(8,128)(2,1)} %bitcast.1, bf16[16,320]{1,0:T(8,128)(2,1)} %project_hbm.1, bf16[3,3,320,320]{3,2,1,0:T(8,128)(2,1)} %conv_one_hbm.1, ...), custom_call_target="tpu_custom_call" | custom-call | tf_op jit(solution)/shard_map/pallas_call | solution.py:537
  27.4 1.6 %copy.12 = f32[1,16,8,256]{3,2,1,0:T(8,128)} copy(f32[1,16,8,256]{3,2,1,0:T(8,128)} %shard_map.82) | data formatting | bytes 262144

commit v3 on v2

--- a/solution.py
+++ b/solution.py
@@ -30,8 +30,8 @@
     tiles,
     x_hbm,
     embed_hbm,
-    scale_ref,
-    decay_ref,
+    scale_hbm,
+    decay_hbm,
     lift_hbm,
     project_hbm,
     conv_one_hbm,
@@ -41,6 +41,8 @@
     embed_ref,
     lift_ref,
     project_ref,
+    scale_ref,
+    decay_ref,
     raw_one,
     raw_two,
     u_one,
@@ -79,11 +81,11 @@
     has_down = space < tiles - 1
 
     pairs = [(x_hbm, x_ref), (embed_hbm, embed_ref), (lift_hbm, lift_ref)]
-    pairs += [(project_hbm, project_ref)]
+    pairs += [(project_hbm, project_ref), (scale_hbm, scale_ref), (decay_hbm, decay_ref)]
     pairs += [(conv_one_hbm.at[p], raw_one.at[p]) for p in range(3)]
     pairs += [(conv_two_hbm.at[p], raw_two.at[p]) for p in range(3)]
     loads = [pltpu.make_async_copy(a, b, load_sem.at[i]) for i, (a, b) in enumerate(pairs)]
-    for load in loads[:7]:
+    for load in loads[:9]:
         load.start()
 
     barrier = pltpu.get_barrier_semaphore()
@@ -299,23 +301,31 @@
         ] + [last]
 
     def weight_items(raw, weight, number):
-        def item(p):
-            loads[number + p].wait()
-            taps = [raw[p, q].astype(jnp.float32) for q in range(3)]
-            outer = taps[0] + taps[2]
+        def item(p, start):
+            if start == 0:
+                loads[number + p].wait()
+            lines = slice(start, start + chunk)
+            taps = [raw[p, q, lines] for q in range(3)]
+            centre = taps[1].astype(jnp.float32)
+            outer = taps[0].astype(jnp.float32) + taps[2].astype(jnp.float32)
             filtered = (
-                0.5 * taps[0],
-                0.25 * (outer + taps[1]),
-                0.25 * (outer - taps[1]),
-                0.5 * taps[2],
+                half_of * taps[0],
+                quarter * (outer + centre).astype(jnp.bfloat16),
+                quarter * (outer - centre).astype(jnp.bfloat16),
+                half_of * taps[2],
             )
             for m, value in enumerate(filtered):
-                value = value.astype(jnp.bfloat16)
-                weight[m, :, p * main : (p + 1) * main] = value[:, :main]
+                weight[m, lines, p * main : (p + 1) * main] = value[:, :main]
                 place = 3 * main + p * rest
-                weight[m, :, place : place + rest] = value[:, main:]
-
-        return [functools.partial(item, p) for p in range(3)]
+                weight[m, lines, place : place + rest] = value[:, main:]
+
+        half_of = jnp.asarray(0.5, jnp.bfloat16)
+        quarter = jnp.asarray(0.25, jnp.bfloat16)
+        return [
+            functools.partial(item, p, start)
+            for p in range(3)
+            for start in range(0, feats, chunk)
+        ]
 
     reached = set()
 
@@ -398,7 +408,11 @@
 
         for sweep, pair in missing(0):
             run(build_items(sweep, pair))
-        run(weight_items(raw_one, u_one, 4))
+        greeted = (steps - 1) + jnp.where(has_up, 1, 0) + jnp.where(has_down, 1, 0)
+        pl.semaphore_wait(barrier, greeted)
+        send_up(0)
+        send_down(0)
+        run(weight_items(raw_one, u_one, 6))
         after = []
         waiting = []
         for place, (sweep, kind, pair) in enumerate(turns):
@@ -409,14 +423,14 @@
             for coming in missing(place + 1):
                 late += build_items(*coming)
             if place == 0:
-                waiting = weight_items(raw_two, u_two, 7)
-                loads[7].start()
-                loads[8].start()
-                loads[9].start()
+                waiting = weight_items(raw_two, u_two, 9)
+                for load in loads[9:]:
+                    load.start()
             elif place + 1 < len(turns) and turns[place + 1][1] == "B":
                 late, waiting = late + waiting, []
             else:
-                late, waiting = late + waiting[:1], waiting[1:]
+                many = len(waiting) // 2
+                late, waiting = late + waiting[:many], waiting[many:]
             if kind == "A":
                 products = [
                     functools.partial(product, u_one, main_one, rest_one, m, pair, sweep)
@@ -458,11 +472,7 @@
         rows_f32[row] = value
         state_rows[row] = value
         xb_rows[0, row + 2] = value.astype(jnp.bfloat16)
-    greeted = (steps - 1) + jnp.where(has_up, 1, 0) + jnp.where(has_down, 1, 0)
-    pl.semaphore_wait(barrier, greeted)
-    send_up(0)
-    send_down(0)
-    for load in loads[1:4]:
+    for load in loads[1:6]:
         load.wait()
     wide = (-feats) % 128
     parts = [
@@ -531,19 +541,21 @@
         lines = pl.cdiv(depth + EXTRA, 128)
         wide = (lines + 1 - lines % 2) * 128
         peers = max(steps - 1, 1)
+        room = 4 * chans * height * width
         vmem = pl.BlockSpec(memory_space=pltpu.VMEM)
-        smem = pl.BlockSpec(memory_space=pltpu.SMEM)
         hbm = pl.BlockSpec(memory_space=pltpu.HBM)
         return pl.pallas_call(
             functools.partial(kernel, steps, tiles),
-            out_shape=jax.ShapeDtypeStruct((1, chans, height, width), jnp.float32),
-            in_specs=[hbm, hbm, smem, smem, hbm, hbm, hbm, hbm],
+            out_shape=pltpu.VMEM((1, chans, height, width), jnp.float32),
+            in_specs=[hbm] * 8,
             out_specs=vmem,
             scratch_shapes=[
                 pltpu.VMEM((chans, height, width), jnp.float32),
                 pltpu.VMEM((1, feats), jnp.float32),
                 pltpu.VMEM((chans, feats), jnp.bfloat16),
                 pltpu.VMEM((chans, feats), jnp.bfloat16),
+                pltpu.SMEM((1,), jnp.float32),
+                pltpu.SMEM((1,), jnp.float32),
                 pltpu.VMEM((3, 3, feats, feats), jnp.bfloat16),
                 pltpu.VMEM((3, 3, feats, feats), jnp.bfloat16),
                 pltpu.VMEM((4, feats, wide), jnp.bfloat16),
@@ -563,14 +575,14 @@
                 pltpu.VMEM((height, chans, width), jnp.float32),
                 pltpu.VMEM((ITERS, height, chans, width), jnp.bfloat16),
                 pltpu.VMEM((ITERS, peers, height, chans, width), jnp.bfloat16),
-                pltpu.SemaphoreType.DMA((10,)),
+                pltpu.SemaphoreType.DMA((12,)),
                 pltpu.SemaphoreType.DMA((ITERS, 2)),
                 pltpu.SemaphoreType.DMA((ITERS, 2)),
                 pltpu.SemaphoreType.DMA((ITERS, peers, height // 2)),
                 pltpu.SemaphoreType.DMA((ITERS, peers, height // 2)),
             ],
             compiler_params=pltpu.CompilerParams(
-                collective_id=0, has_side_effects=True, vmem_limit_bytes=67043328
+                collective_id=0, has_side_effects=True, vmem_limit_bytes=67043328 - room
             ),
         )(
             first_state,

time: 29.3 us -> 26.6 us (0.908)
  Pallas kernels: 26.1 us -> 24.5 us
  local copies, waits for them, and re-layouts: 1.57 us -> 0.66 us
    pallas_call x1, Pallas kernels: 26.1 us -> 24.5 us  [per_device(): pl.pallas_call(functools.partial(kernel, steps, tiles), out_shape=pltpu.V...]
    unnamed x1, local copies, waits for them, and re-layouts: 1.57 us -> 0.66 us
where the time goes in v3:
time: 26.6 us; the launch traced here: 26.4 us
  Pallas kernels  24.5 us (92%)
  between operations  1.31 us (5%)
  local copies, waits for them, and re-layouts  0.66 us (2%)
    pallas_call x1, Pallas kernels, per_device(): pl.pallas_call(functools.partial(kernel, steps, tiles), out_shape=pltpu.V...  24.5 us
    unnamed x1, local copies, waits for them, and re-layouts  0.66 us

profile of v3, /device:TPU:21, one launch (start us, length us, event | category | flops | bytes accessed | tf_op | source)
XLA Modules:
  0.0 26.4 jit_solution(4785708744887121782)
XLA Ops:
  1.3 24.5 %shard_map.82 = f32[1,16,8,256]{3,2,1,0:T(8,128)S(1)} custom-call(f32[16,8,256]{2,1,0:T(8,128)} %x_hbm.1, f32[1,320]{1,0:T(1,128)} %embed_hbm.1, f32[1]{0:T(128)S(6)} %copy.11.scale_hbm, f32[1]{0:T(128)S(6)} %copy.12.decay_hbm, bf16[16,320]{1,0:T(8,128)(2,1)} %bitcast.1, bf16[16,320]{1,0:T(8,128)(2,1)} %project_hbm.1, bf16[3,3,320,320]{3,2,1,0:T(8,128)(2,1)} %conv_one_hbm.1, ...), custom_call_target="tpu_custom_call" | custom-call | tf_op jit(solution)/shard_map/pallas_call | solution.py:547
  25.8 0.7 %copy.10 = f32[1,16,8,256]{3,2,1,0:T(8,128)} copy(f32[1,16,8,256]{3,2,1,0:T(8,128)S(1)} %shard_map.82) | data formatting | bytes 262144

commit v4 on v3

--- a/solution.py
+++ b/solution.py
@@ -195,7 +195,7 @@
         xb = xb_rows[sweep, index]
         return jnp.concatenate([xb[:, side:] if odd else xb[:, :side], ones], axis=0)
 
-    def product(weight, mains, rests, m, pair, sweep=None):
+    def product(weight, mains, rests, m, pair, sweep=None, part=None):
         taken = []
         used = depth + EXTRA
         for index in pair:
@@ -209,7 +209,7 @@
                 pieces.append(jnp.zeros((EXTRA, side), jnp.bfloat16))
             taken.append(jnp.concatenate(pieces, axis=0))
         return jnp.dot(
-            weight[m, :, :used],
+            weight[m, part, :used],
             jnp.concatenate(taken, axis=1),
             preferred_element_type=jnp.float32,
         )
@@ -300,10 +300,8 @@
             for start in range(0, feats, chunk)
         ] + [last]
 
-    def weight_items(raw, weight, number):
+    def weight_items(raw, weight):
         def item(p, start):
-            if start == 0:
-                loads[number + p].wait()
             lines = slice(start, start + chunk)
             taps = [raw[p, q, lines] for q in range(3)]
             centre = taps[1].astype(jnp.float32)
@@ -367,6 +365,12 @@
         for item in items:
             item()
 
+    def mixed(some, others):
+        whole = list(some)
+        for place, item in enumerate(others):
+            whole.insert((place + 1) * (len(some) + len(others)) // (len(others) + 1), item)
+        return whole
+
     def turn(slot, products, early, late):
         count = len(products)
         shares = [[] for _ in products]
@@ -374,9 +378,13 @@
             shares[place * (count - 1) // len(early)].append(item)
         for place, item in enumerate(late):
             shares[count // 2 + place * (count // 2) // len(late)].append(item)
+        size = feats // 2
         for m, make in enumerate(products):
-            prods[slot, m] = make()
-            run(shares[m])
+            for place in range(2):
+                lines = slice(place * size, (place + 1) * size)
+                prods[slot, m, lines] = make(part=lines)
+                some = len(shares[m]) // 2
+                run(shares[m][some:] if place else shares[m][:some])
 
     def plan():
         top = height // 2 - 1
@@ -412,7 +420,11 @@
         pl.semaphore_wait(barrier, greeted)
         send_up(0)
         send_down(0)
-        run(weight_items(raw_one, u_one, 6))
+        for load in loads[6:9]:
+            load.wait()
+        for load in loads[9:]:
+            load.start()
+        run(weight_items(raw_one, u_one))
         after = []
         waiting = []
         for place, (sweep, kind, pair) in enumerate(turns):
@@ -422,15 +434,15 @@
             late = []
             for coming in missing(place + 1):
                 late += build_items(*coming)
-            if place == 0:
-                waiting = weight_items(raw_two, u_two, 9)
+            if place == 1:
                 for load in loads[9:]:
-                    load.start()
-            elif place + 1 < len(turns) and turns[place + 1][1] == "B":
-                late, waiting = late + waiting, []
-            else:
-                many = len(waiting) // 2
-                late, waiting = late + waiting[:many], waiting[many:]
+                    load.wait()
+                waiting = weight_items(raw_two, u_two)
+                late = mixed(late, waiting[:5])
+                after = mixed(after, waiting[5:7])
+            if place == 2:
+                late = mixed(late, waiting[7:12])
+                after = mixed(after, waiting[12:])
             if kind == "A":
                 products = [
                     functools.partial(product, u_one, main_one, rest_one, m, pair, sweep)

time: 26.6 us -> 25.7 us (0.966)
  Pallas kernels: 24.5 us -> 23.5 us
    pallas_call x1, Pallas kernels: 24.5 us -> 23.5 us  [per_device(): pl.pallas_call(functools.partial(kernel, steps, tiles), out_shape=pltpu.V...]
where the time goes in v4:
time: 25.7 us; the launch traced here: 25.5 us
  Pallas kernels  23.5 us (91%)
  between operations  1.31 us (5%)
  local copies, waits for them, and re-layouts  0.66 us (3%)
    pallas_call x1, Pallas kernels, per_device(): pl.pallas_call(functools.partial(kernel, steps, tiles), out_shape=pltpu.V...  23.5 us
    unnamed x1, local copies, waits for them, and re-layouts  0.66 us

profile of v4, /device:TPU:21, one launch (start us, length us, event | category | flops | bytes accessed | tf_op | source)
XLA Modules:
  0.0 25.5 jit_solution(13551063278918426270)
XLA Ops:
  1.3 23.5 %shard_map.82 = f32[1,16,8,256]{3,2,1,0:T(8,128)S(1)} custom-call(f32[16,8,256]{2,1,0:T(8,128)} %x_hbm.1, f32[1,320]{1,0:T(1,128)} %embed_hbm.1, f32[1]{0:T(128)S(6)} %copy.11.scale_hbm, f32[1]{0:T(128)S(6)} %copy.12.decay_hbm, bf16[16,320]{1,0:T(8,128)(2,1)} %bitcast.1, bf16[16,320]{1,0:T(8,128)(2,1)} %project_hbm.1, bf16[3,3,320,320]{3,2,1,0:T(8,128)(2,1)} %conv_one_hbm.1, ...), custom_call_target="tpu_custom_call" | custom-call | tf_op jit(solution)/shard_map/pallas_call | solution.py:559
  24.8 0.7 %copy.10 = f32[1,16,8,256]{3,2,1,0:T(8,128)} copy(f32[1,16,8,256]{3,2,1,0:T(8,128)S(1)} %shard_map.82) | data formatting | bytes 262144

commit v5 on v4

--- a/solution.py
+++ b/solution.py
@@ -505,12 +505,15 @@
 
     all_turns()
 
-    for pair in range(height // 2):
+    back = parted(True)
+    for pair in list(range(1, height // 2)) + [0]:
         wait_drift(ITERS - 1, pair)
-    for row in range(height):
-        turned[:, row, :] = drift_own[row] + earlier(ITERS - 1, row)
-    total = reorder(turned[...].reshape(chans * height, width), parted(True))
-    out_ref[0] = x_ref[...] + total.reshape(chans, height, width)
+        rows = (2 * pair, 2 * pair + 1)
+        totals = [drift_own[row] + earlier(ITERS - 1, row) for row in rows]
+        total = reorder(jnp.concatenate(totals, axis=0), back)
+        for place, row in enumerate(rows):
+            part = total[place * chans : (place + 1) * chans]
+            out_ref[0, :, row, :] = x_ref[:, row, :] + part
 
     for sweep in range(ITERS):
         up, down = halo_copies(sweep)

time: 25.7 us -> 25.5 us (level)
  no operation moved by 1% of the time
where the time goes in v5:
time: 25.5 us; the launch traced here: 25.4 us
  Pallas kernels  23.4 us (92%)
  between operations  1.31 us (5%)
  local copies, waits for them, and re-layouts  0.66 us (3%)
    pallas_call x1, Pallas kernels, per_device(): pl.pallas_call(functools.partial(kernel, steps, tiles), out_shape=pltpu.V...  23.4 us
    unnamed x1, local copies, waits for them, and re-layouts  0.66 us

profile of v5, /device:TPU:21, one launch (start us, length us, event | category | flops | bytes accessed | tf_op | source)
XLA Modules:
  0.0 25.4 jit_solution(14149459671299427407)
XLA Ops:
  1.3 23.4 %shard_map.82 = f32[1,16,8,256]{3,2,1,0:T(8,128)S(1)} custom-call(f32[16,8,256]{2,1,0:T(8,128)} %x_hbm.1, f32[1,320]{1,0:T(1,128)} %embed_hbm.1, f32[1]{0:T(128)S(6)} %copy.11.scale_hbm, f32[1]{0:T(128)S(6)} %copy.12.decay_hbm, bf16[16,320]{1,0:T(8,128)(2,1)} %bitcast.1, bf16[16,320]{1,0:T(8,128)(2,1)} %project_hbm.1, bf16[3,3,320,320]{3,2,1,0:T(8,128)(2,1)} %conv_one_hbm.1, ...), custom_call_target="tpu_custom_call" | custom-call | tf_op jit(solution)/shard_map/pallas_call | solution.py:562
  24.7 0.7 %copy.10 = f32[1,16,8,256]{3,2,1,0:T(8,128)} copy(f32[1,16,8,256]{3,2,1,0:T(8,128)S(1)} %shard_map.82) | data formatting | bytes 262144
